TPU v7x, 32 devices: a whole 2x2x4 slice. The times are simulated.
32 devices in a mesh: ctx: 8 (over y, x, core), fsdp: 4 (over z).
Axes of the slice: x: 2, y: 2, z: 4, core: 2. Of those that a mesh axis runs over, the one named last changes fastest.
Arguments:
- hidden_in: bfloat16 [4, 1024, 2048], P('fsdp', 'ctx'), may hold values from -18 to 18
- out_grad: bfloat16 [4, 1024, 2048], P('fsdp', 'ctx'), may hold values from -6 to 6
- positions: int32 [4, 1024], P('fsdp', 'ctx'), may hold values from 0 to 1023, as said below
- block_order: int32 [16], replicated, may hold values from 0 to 15, as said below
- attn_gain: float32 [2048], replicated, may hold values from 0.25 to 1.75
- ffn_gain: float32 [2048], replicated, may hold values from 0.25 to 1.75
- qkv_weight: bfloat16 [2048, 3072], P('fsdp'), may hold values from -1 to 1
- out_weight: bfloat16 [2048, 2048], P('fsdp'), may hold values from -0.5 to 0.5
- ffn_weight: bfloat16 [2048, 3, 8192], P(None, None, 'fsdp'), may hold values from -0.125 to 0.125
Outputs:
- hidden_out: bfloat16 [4, 1024, 2048], P('fsdp', 'ctx')
- input_grad: float32 [4, 1024, 2048], P('fsdp', 'ctx')
- qkv_weight_grad: float32 [2048, 3072], P(('ctx', 'fsdp'))
- out_weight_grad: float32 [2048, 2048], P(('ctx', 'fsdp'))
- ffn_weight_grad: float32 [2048, 3, 8192], P('ctx', None, 'fsdp')
- attn_gain_grad: float32 [2048], P(('ctx', 'fsdp'))
- ffn_gain_grad: float32 [2048], P(('ctx', 'fsdp'))
Inputs may be any that keep to these rules, and one draw needn't show every extreme that they name: `block_order`: the two slots 2c and 2c + 1 hold two blocks whose numbers add up to 15, and every block number appears once. In initial token order, a sequence's positions rise by one from token to token and restart at 0 at its first token and at the start of each packed document; the first sequence is a single document; they are listed in storage order.
All inputs are finite; a program needn't handle non-finite values.
Results may differ from a plain program's by a relative error of at most 0.03.
Values may be sent and summed in bfloat16 or wider, within the bound.
No kernel may reach another device: no remote copies, remote signals or barrier semaphores. Data moves between devices by JAX's collectives and lax.ppermute only.
A program may use at most 576 MiB of HBM per device.

v0:
```python
import math
import jax
import jax.numpy as jnp
from jax import lax
from jax.sharding import PartitionSpec as P

H = 32
KV = 8
HD = 64
NORM_EPS = 1e-05
ROPE_BASE = 500000.0
block_rows = 512


def rotate(values, token_places):
    head_dim = values.shape[-1]
    half_dim = head_dim // 2
    frequency = jnp.power(ROPE_BASE, -(jnp.arange(half_dim, dtype=jnp.float32) * 2.0 / head_dim))
    angles = token_places.astype(jnp.float32)[:, None] * frequency[None, :]
    cosine = jnp.concatenate([jnp.cos(angles), jnp.cos(angles)], axis=-1)[:, None, :]
    sine_part = jnp.concatenate([jnp.sin(angles), jnp.sin(angles)], axis=-1)[:, None, :]
    turned = jnp.concatenate([-values[..., half_dim:], values[..., :half_dim]], axis=-1)
    return values * cosine + turned * sine_part


def norm_scale(values):
    return lax.rsqrt(jnp.mean(values * values, axis=-1, keepdims=True) + NORM_EPS)


def lookup(entries, row_ids):
    matches = row_ids[:, None] == jnp.arange(entries.shape[0], dtype=jnp.int32)[None, :]
    return jnp.sum(jnp.where(matches, entries[None, :], 0), axis=1)


def anchor_rows(block_order, first_row, row_count, block_len):
    row_ids = first_row + jnp.arange(row_count, dtype=jnp.int32)
    return lookup(block_order, row_ids // block_len) * block_len + row_ids % block_len


def sweep_keys(step_fn, carried, pieces):
    row_count = pieces[0].shape[0]
    full_blocks = row_count // block_rows

    def loop_step(step_index, carry_state):
        key_pair = tuple(
            (
                lax.dynamic_slice_in_dim(piece_rows, step_index * block_rows, block_rows, 0)
                for piece_rows in pieces
            )
        )
        return step_fn(carry_state, key_pair, step_index * block_rows)

    carried = lax.fori_loop(0, full_blocks, loop_step, carried)
    return carried


def body(
    hidden_in,
    out_grad,
    positions,
    block_order,
    attn_gain,
    ffn_gain,
    qkv_weight,
    out_weight,
    ffn_weight,
):
    local_rows = hidden_in.shape[1]
    block_len = local_rows // 2
    ctx_count = lax.axis_size("ctx")
    seq_rows = local_rows * ctx_count
    groups = H // KV
    score_scale = 1.0 / math.sqrt(HD)
    slot_first = 2 * lax.axis_index("ctx") * block_len
    own_anchor = anchor_rows(block_order, slot_first, local_rows, block_len)
    inputs = hidden_in[0].astype(jnp.float32)
    grad_in = out_grad[0]
    token_places = positions[0]
    scale_one = norm_scale(inputs)
    normed_one = (inputs * scale_one * attn_gain).astype(jnp.bfloat16)
    qkv_full, out_full = (
        lax.all_gather(qkv_weight, "fsdp", axis=0, tiled=True),
        lax.all_gather(out_weight, "fsdp", axis=0, tiled=True),
    )
    projected = jnp.dot(normed_one, qkv_full, preferred_element_type=jnp.float32)
    queries = rotate(projected[:, : H * HD].reshape(local_rows, H, HD), token_places).astype(
        jnp.bfloat16
    )
    queries = queries.reshape(local_rows, KV, groups, HD)
    key_local = rotate(
        projected[:, H * HD : (H + KV) * HD].reshape(local_rows, KV, HD), token_places
    ).astype(jnp.bfloat16)
    key_local = key_local.reshape(local_rows, KV * HD)
    value_local = projected[:, (H + KV) * HD :].astype(jnp.bfloat16)

    def masked_scores(key_heads, first_row, row_count):
        scores = (
            jnp.einsum("tkgd,skd->kgts", queries, key_heads, preferred_element_type=jnp.float32)
            * score_scale
        )
        allowed = (
            anchor_rows(block_order, first_row, row_count, block_len)[None, :]
            <= own_anchor[:, None]
        )[None, None]
        return (jnp.where(allowed, scores, -1e30), allowed)

    def forward_step(carry_state, key_pair, first_row):
        top_old, total_old, summed = carry_state
        key_part, value_part = key_pair
        row_count = key_part.shape[0]
        key_heads = key_part.reshape(row_count, KV, HD)
        value_heads = value_part.reshape(row_count, KV, HD)
        scores, allowed = masked_scores(key_heads, first_row, row_count)
        top_new = jnp.maximum(top_old, jnp.max(scores, axis=-1))
        weights = jnp.where(allowed, jnp.exp(scores - top_new[..., None]), 0.0)
        rescale = jnp.exp(top_old - top_new)
        total_new = total_old * rescale + jnp.sum(weights, axis=-1)
        summed = summed * rescale[..., None] + jnp.einsum(
            "kgts,skd->kgtd",
            weights.astype(jnp.bfloat16),
            value_heads,
            preferred_element_type=jnp.float32,
        )
        return (top_new, total_new, summed)

    start_state = (
        jnp.full((KV, groups, local_rows), -1e30, jnp.float32),
        jnp.zeros((KV, groups, local_rows), jnp.float32),
        jnp.zeros((KV, groups, local_rows, HD), jnp.float32),
    )
    attn_state = sweep_keys(
        forward_step,
        start_state,
        (
            lax.all_gather(key_local, "ctx", axis=0, tiled=True),
            lax.all_gather(value_local, "ctx", axis=0, tiled=True),
        ),
    )
    row_top, row_total, summed = attn_state
    log_total = row_top + jnp.log(row_total)
    attended = (summed / row_total[..., None]).transpose(2, 0, 1, 3)
    attn_rows = attended.reshape(local_rows, H * HD).astype(jnp.bfloat16)
    residual = inputs + jnp.einsum(
        "tc,dc->td", attn_rows, out_full, preferred_element_type=jnp.float32
    )
    scale_two = norm_scale(residual)
    normed_two = (residual * scale_two * ffn_gain).astype(jnp.bfloat16)
    rows_in, rows_out = (
        lax.all_gather(normed_two, "fsdp", axis=0, tiled=True),
        lax.all_gather(grad_in, "fsdp", axis=0, tiled=True),
    )
    weight_piece = lax.all_gather(ffn_weight, "fsdp", axis=2, tiled=True)
    gate_part = jnp.dot(normed_two, weight_piece[:, 0, :], preferred_element_type=jnp.float32)
    up_part = jnp.dot(normed_two, weight_piece[:, 1, :], preferred_element_type=jnp.float32)
    act_part = (gate_part * jax.nn.sigmoid(gate_part) * up_part).astype(jnp.bfloat16)
    out_sum = jnp.einsum(
        "tf,df->td", act_part, weight_piece[:, 2, :], preferred_element_type=jnp.float32
    )
    gate_all = gate_part
    up_all = up_part
    gate_pre = gate_all
    up_pre = up_all
    activated = act_part
    weight_piece = lax.all_gather(ffn_weight, "fsdp", axis=2, tiled=True)
    row_count = weight_piece.shape[2]
    gate_part = gate_pre
    up_part = up_pre
    sig_part = jax.nn.sigmoid(gate_part)
    act_part_grad = jnp.dot(grad_in, weight_piece[:, 2, :], preferred_element_type=jnp.float32)
    gate_part_grad = (
        act_part_grad * up_part * sig_part * (1.0 + gate_part * (1.0 - sig_part))
    ).astype(jnp.bfloat16)
    up_part_grad = (act_part_grad * gate_part * sig_part).astype(jnp.bfloat16)
    sum_grad = jnp.einsum(
        "tf,df->td", gate_part_grad, weight_piece[:, 0, :], preferred_element_type=jnp.float32
    )
    sum_grad = sum_grad + jnp.einsum(
        "tf,df->td", up_part_grad, weight_piece[:, 1, :], preferred_element_type=jnp.float32
    )
    gate_all = gate_part_grad
    up_all = up_part_grad
    gate_grad = gate_all
    up_grad = up_all
    gate_grad, up_grad, activated = (
        lax.all_to_all(gate_grad, "fsdp", split_axis=1, concat_axis=0, tiled=True),
        lax.all_to_all(up_grad, "fsdp", split_axis=1, concat_axis=0, tiled=True),
        lax.all_to_all(activated, "fsdp", split_axis=1, concat_axis=0, tiled=True),
    )
    output = (residual + out_sum).astype(jnp.bfloat16)
    ffn_weight_grad = lax.psum_scatter(
        jnp.stack(
            [
                jnp.einsum("tc,tf->cf", rows_in, gate_grad, preferred_element_type=jnp.float32),
                jnp.einsum("tc,tf->cf", rows_in, up_grad, preferred_element_type=jnp.float32),
                jnp.einsum("tc,tf->cf", rows_out, activated, preferred_element_type=jnp.float32),
            ],
            axis=1,
        ).astype(jnp.bfloat16),
        "ctx",
        scatter_dimension=0,
        tiled=True,
    ).astype(jnp.float32)
    unit_two = residual * scale_two
    ffn_gain_term = jnp.sum(sum_grad * unit_two, axis=0)
    scaled_two = ffn_gain * sum_grad
    residual_grad = grad_in.astype(jnp.float32) + scale_two * (
        scaled_two - unit_two * jnp.mean(scaled_two * unit_two, axis=-1, keepdims=True)
    )
    residual_bf = residual_grad.astype(jnp.bfloat16)
    attn_grad = jnp.dot(residual_bf, out_full, preferred_element_type=jnp.float32).astype(
        jnp.bfloat16
    )
    out_term = jnp.einsum("td,tc->dc", residual_bf, attn_rows, preferred_element_type=jnp.float32)
    attn_grad_heads = attn_grad.reshape(local_rows, KV, groups, HD)
    row_delta = jnp.sum(attn_grad_heads.astype(jnp.float32) * attended, axis=-1).transpose(1, 2, 0)

    def backward_step(carry_state, key_pair, first_row):
        query_grad, key_grad, value_grad = carry_state
        key_part, value_part = key_pair
        row_count = key_part.shape[0]
        key_heads = key_part.reshape(row_count, KV, HD)
        value_heads = value_part.reshape(row_count, KV, HD)
        scores, allowed = masked_scores(key_heads, first_row, row_count)
        probs = jnp.where(allowed, jnp.exp(scores - log_total[..., None]), 0.0)
        value_piece = jnp.einsum(
            "kgts,tkgd->skd",
            probs.astype(jnp.bfloat16),
            attn_grad_heads,
            preferred_element_type=jnp.float32,
        )
        prob_grad = jnp.einsum(
            "tkgd,skd->kgts", attn_grad_heads, value_heads, preferred_element_type=jnp.float32
        )
        score_grad = (probs * (prob_grad - row_delta[..., None]) * score_scale).astype(jnp.bfloat16)
        query_grad = query_grad + jnp.einsum(
            "kgts,skd->tkgd", score_grad, key_heads, preferred_element_type=jnp.float32
        )
        key_piece = jnp.einsum(
            "kgts,tkgd->skd", score_grad, queries, preferred_element_type=jnp.float32
        )
        key_grad = lax.dynamic_update_slice_in_dim(
            key_grad, key_piece.reshape(row_count, KV * HD), first_row, 0
        )
        value_grad = lax.dynamic_update_slice_in_dim(
            value_grad, value_piece.reshape(row_count, KV * HD), first_row, 0
        )
        return (query_grad, key_grad, value_grad)

    start_grads = (
        jnp.zeros((local_rows, KV, groups, HD), jnp.float32),
        jnp.zeros((seq_rows, KV * HD), jnp.float32),
        jnp.zeros((seq_rows, KV * HD), jnp.float32),
    )
    grad_state = sweep_keys(
        backward_step,
        start_grads,
        (
            lax.all_gather(key_local, "ctx", axis=0, tiled=True),
            lax.all_gather(value_local, "ctx", axis=0, tiled=True),
        ),
    )
    query_grad, key_grad_all, value_grad_all = grad_state
    key_grad_own, value_grad_own = (
        lax.psum_scatter(
            key_grad_all.astype(jnp.bfloat16), "ctx", scatter_dimension=0, tiled=True
        ).astype(jnp.float32),
        lax.psum_scatter(
            value_grad_all.astype(jnp.bfloat16), "ctx", scatter_dimension=0, tiled=True
        ).astype(jnp.float32),
    )
    projected_grad = jnp.concatenate(
        [
            rotate(query_grad.reshape(local_rows, H, HD), -token_places).reshape(
                local_rows, H * HD
            ),
            rotate(key_grad_own.reshape(local_rows, KV, HD), -token_places).reshape(
                local_rows, KV * HD
            ),
            value_grad_own,
        ],
        axis=1,
    ).astype(jnp.bfloat16)
    normed_one_grad = jnp.einsum(
        "tc,dc->td", projected_grad, qkv_full, preferred_element_type=jnp.float32
    )
    qkv_term = jnp.einsum(
        "td,tc->dc", normed_one, projected_grad, preferred_element_type=jnp.float32
    )
    unit_one = inputs * scale_one
    attn_gain_term = jnp.sum(normed_one_grad * unit_one, axis=0)
    scaled_one = attn_gain * normed_one_grad
    input_grad = residual_grad + scale_one * (
        scaled_one - unit_one * jnp.mean(scaled_one * unit_one, axis=-1, keepdims=True)
    )
    qkv_grad, out_weight_grad, attn_gain_grad, ffn_gain_grad = (
        lax.psum_scatter(qkv_term, ("ctx", "fsdp"), scatter_dimension=0, tiled=True),
        lax.psum_scatter(out_term, ("ctx", "fsdp"), scatter_dimension=0, tiled=True),
        lax.psum_scatter(attn_gain_term, ("ctx", "fsdp"), scatter_dimension=0, tiled=True),
        lax.psum_scatter(ffn_gain_term, ("ctx", "fsdp"), scatter_dimension=0, tiled=True),
    )
    return (
        output[None],
        input_grad[None],
        qkv_grad,
        out_weight_grad,
        ffn_weight_grad,
        attn_gain_grad,
        ffn_gain_grad,
    )


def solution(mesh):
    return jax.shard_map(
        body,
        mesh=mesh,
        in_specs=(
            P("fsdp", "ctx", None),
            P("fsdp", "ctx", None),
            P("fsdp", "ctx"),
            P(),
            P(),
            P(),
            P("fsdp", None),
            P("fsdp", None),
            P(None, None, "fsdp"),
        ),
        out_specs=(
            P("fsdp", "ctx", None),
            P("fsdp", "ctx", None),
            P(("ctx", "fsdp"), None),
            P(("ctx", "fsdp"), None),
            P("ctx", None, "fsdp"),
            P(("ctx", "fsdp")),
            P(("ctx", "fsdp")),
        ),
        check_vma=False,
    )
```

profile of v0, /device:TPU:0, one launch (start us, length us, event | category | flops | bytes accessed | tf_op | source)
XLA Modules:
  0.0 3142.8 jit_solution(4543832504179743126)
XLA Ops:
  10.9 219.6 %all-gather.9.cloned.1.call-done = bf16[2048,3072]{1,0:T(8,128)(2,1)} async-done(((bf16[512,3072]{1,0:T(8,128)(2,1)}), bf16[2048,3072]{1,0:T(8,128)(2,1)}) %all-gather.9.cloned.1.call-update) | async-done | bytes 12582928 | tf_op jit(solution)/shard_map/all_gather | solution.py:82
  230.5 6.7 fusion.70
  241.2 18.8 all-gather.11.cloned.1.call-done
  261.5 24.4 all-gather.13.cloned.1.call-done
  287.4 33.5 %while.40 = (s32[]{:T(128)}, f32[8,4,128]{2,1,0:T(4,128)S(1)}, f32[8,4,128]{2,1,0:T(4,128)S(1)}, f32[8,4,128,64]{2,3,1,0:T(8,128)}, s32[16]{0:T(128)S(1)}, /*ind...) while((s32[]{:T(128)}, f32[8,4,128]{2,1,0:T(4,128)S(1)}, ...), condition=%wide.region_6.7_spmd.clone, body=%wide.region_2.6_spmd.clone.sunk | while | flops 565045760 | bytes 65024804 | solution.py:53
  293.1 5.8 fusion.136
  323.4 113.5 %all-gather.15.cloned.1.call-done = bf16[2048,2048]{1,0:T(8,128)(2,1)} async-done(((bf16[512,2048]{1,0:T(8,128)(2,1)}), bf16[2048,2048]{1,0:T(8,128)(2,1)}) %all-gather.15.cloned.1.call-update) | async-done | bytes 8388624 | tf_op jit(solution)/shard_map/all_gather | solution.py:83
  436.9 6.5 multiply_reduce_fusion.2
  446.2 1650.2 %all-gather.17.cloned.1.call-done = bf16[2048,3,8192]{2,0,1:T(8,128)(2,1)} async-done(((bf16[2048,3,2048]{2,0,1:T(8,128)(2,1)}), bf16[2048,3,8192]{2,0,1:T(8,128)(2,1)}) %all-gather.17.cloned.1.call-update) | async-done | bytes 100663312 | tf_op jit(solution)/shard_map/all_gather | solution.py:152
  2096.4 15.5 fusion.36
  2112.0 15.2 fusion.38
  2127.1 17.6 multiply_convert_fusion
  2152.3 17.3 fusion.35
  2169.7 20.1 multiply_reduce_fusion
  2204.1 29.0 all-to-all-done.1
  2240.0 40.3 %while.41 = (s32[]{:T(128)}, f32[128,8,4,64]{0,3,2,1:T(8,128)S(1)}, bf16[1024,512]{0,1:T(8,128)(2,1)}, bf16[1024,512]{0,1:T(8,128)(2,1)}, bf16[1024,512]{0,1:T(8...) while((s32[]{:T(128)}, f32[128,8,4,64]{0,3,2,1:T(8,128)S(1)}, ...), condition=%wide.region_12.13_spmd.clone, body=%wide.region_10.12_spmd.clone.sunk | while | flops 1370069504 | bytes 124515376 | solution.py:53
  2242.5 6.0 fusion.151
  2251.7 5.6 fusion.153
  2262.7 6.0 fusion.151
  2292.8 10.4 convert_bitcast_fusion.1
  2303.2 8.5 convert_bitcast_fusion.2
  2311.7 27.3 all-to-all-done.2
  2339.1 10.1 convert_bitcast_fusion
  2349.2 14.2 pad_maximum_fusion
  2364.7 11.5 fusion.66
  2379.9 16.4 fusion.63
  2397.6 17.3 fusion.44
  2414.9 9.4 fusion.56
  2424.3 39.6 %all-reduce.2 = (f32[2048]{0:T(1024)S(1)}, f32[2048]{0:T(1024)S(1)}) all-reduce(f32[2048]{0:T(1024)S(1)} %get-tuple-element.684, f32[2048]{0:T(1024)S(1)} %copy-done.33), channel_id=8, replica_groups=mesh['ctx'=8,'fsdp'=4] {'ctx','fsdp'}, use_global_device_ids=true, to_apply=%region_20.21.clone | all-reduce | flops 4096 | bytes 32768
  2466.4 54.5 %reduce-scatter.14.cloned.1.call-done = bf16[256,3,2048]{2,0,1:T(8,128)(2,1)} async-done(((bf16[2048,3,2048]{2,0,1:T(8,128)(2,1)}), bf16[256,3,2048]{2,0,1:T(8,128)(2,1)}) %reduce-scatter.14.cloned.1.call-update) | async-done | bytes 3145744 | tf_op jit(solution)/shard_map/reduce_scatter | solution.py:190
  2526.3 358.1 %reduce-scatter.12.cloned.1.call-done = f32[64,2048]{1,0:T(8,128)} async-done(((f32[2048,2048]{1,0:T(8,128)}), f32[64,2048]{1,0:T(8,128)}) %reduce-scatter.12.cloned.1.call-update) | async-done | bytes 524304 | tf_op jit(solution)/shard_map/reduce_scatter | solution.py:297
  2884.4 251.3 %reduce-scatter.10.cloned.1.call-done = f32[64,3072]{1,0:T(8,128)} async-done(((f32[2048,3072]{1,0:T(8,128)}), f32[64,3072]{1,0:T(8,128)}) %reduce-scatter.10.cloned.1.call-update) | async-done | bytes 786448 | tf_op jit(solution)/shard_map/reduce_scatter | solution.py:296
  (225 shorter events, 121.2 us)
Async XLA Ops:
  7.2 223.3 %all-gather.9.cloned.1.call-start = ((), (), s32[]{:S(2)}) async-start(), calls=%async_computation.8 | async-start | bytes 15728640 | tf_op jit(solution)/shard_map/all_gather | solution.py:82
  7.9 252.1 %all-gather.11.cloned.1.call-start = ((), (), s32[]{:S(2)}) async-start(), calls=%async_computation.9 | async-start | bytes 1179648 | tf_op jit(solution)/shard_map/all_gather | solution.py:135
  10.9 226.3 %copy-start.31 = (f32[128]{0:T(128)}, f32[128]{0:T(128)S(1)}, u32[]{:S(2)}) copy-start(f32[128]{0:T(128)S(1)} %add_rsqrt_fusion.1) | copy-start | bytes 1540
  238.3 47.6 %all-gather.13.cloned.1.call-start = ((), (), s32[]{:S(2)}) async-start(), calls=%async_computation.10 | async-start | bytes 1179648 | tf_op jit(solution)/shard_map/all_gather | solution.py:136
  239.0 197.9 %all-gather.15.cloned.1.call-start = ((), (), s32[]{:S(2)}) async-start(), calls=%async_computation.11 | async-start | bytes 10485760 | tf_op jit(solution)/shard_map/all_gather | solution.py:83
  239.6 1856.8 %all-gather.17.cloned.1.call-start = ((), (), s32[]{:S(2)}) async-start(), calls=%async_computation.12 | async-start | bytes 125829120 | tf_op jit(solution)/shard_map/all_gather | solution.py:152
  240.2 2052.6 %all-gather.19.cloned.1.call-start = ((), (), s32[]{:S(2)}) async-start(), calls=%async_computation.15 | async-start | bytes 2621440 | tf_op jit(solution)/shard_map/all_gather | solution.py:149
  287.4 149.6 %copy-start.7 = (bf16[1,128,2048]{2,1,0:T(8,128)(2,1)S(1)}, bf16[1,128,2048]{2,1,0:T(8,128)(2,1)}, u32[]{:S(2)}) copy-start(bf16[1,128,2048]{2,1,0:T(8,128)(2,1)} %param.13) | copy-start | bytes 1572868
  293.1 7.6 copy-start
  320.9 125.3 %copy-start.3 = (bf16[1024,512]{0,1:T(8,128)(2,1)}, bf16[1024,512]{0,1:T(8,128)(2,1)S(1)}, u32[]{:S(2)}) copy-start(bf16[1024,512]{0,1:T(8,128)(2,1)S(1)} %get-tuple-element.1013) | copy-start | bytes 3145732
  320.9 123.6 %copy-start.30 = (f32[2048]{0:T(1024)S(1)}, f32[2048]{0:T(1024)}, u32[]{:S(2)}) copy-start(f32[2048]{0:T(1024)} %param.18) | copy-start | bytes 24580
  445.4 1866.3 %all-gather.21.cloned.1.call-start = ((), (), s32[]{:S(2)}) async-start(), calls=%async_computation.17 | async-start | bytes 2621440 | tf_op jit(solution)/shard_map/all_gather | solution.py:150
  446.2 1665.7 %copy-start.24 = (bf16[128,2048]{1,0:T(8,128)(2,1)S(1)}, bf16[128,2048]{1,0:T(8,128)(2,1)}, u32[]{:S(2)}) copy-start(bf16[128,2048]{1,0:T(8,128)(2,1)} %multiply_convert_fusion.3) | copy-start | bytes 1572868
  2147.6 85.5 %all-to-all-start.1 = ((bf16[128,4,2048]{2,0,1:T(8,128)(2,1)}), bf16[128,4,2048]{2,0,1:T(8,128)(2,1)}, u32[]{:S(2)}, u32[]{:S(2)}) async-start(bf16[128,4,2048]{2,0,1:T(8,128)(2,1)} %bitcast.282), calls=%async_computation.3 | async-start | bytes 4194304 | tf_op jit(solution)/shard_map/all_to_all | solution.py:186
  2169.7 20.1 copy-start.25
  2233.1 53.1 %all-to-all-start = ((bf16[128,4,2048]{2,0,1:T(8,128)(2,1)}), bf16[128,4,2048]{2,0,1:T(8,128)(2,1)}, u32[]{:S(2)}, u32[]{:S(2)}) async-start(bf16[128,4,2048]{2,0,1:T(8,128)(2,1)} %bitcast.280), calls=%async_computation.2 | async-start | bytes 4194304 | tf_op jit(solution)/shard_map/all_to_all | solution.py:185
  2237.5 139.9 %reduce-scatter.16.cloned.1.call-start = ((), (), s32[]{:S(2)}) async-start(), calls=%async_computation.18 | async-start | bytes 1179648
  2251.7 8.5 copy-start.22
  2271.8 7.0 copy-start.14
  2271.9 8.5 copy-start.22
  2280.4 10.6 copy-start.18
  2286.2 52.9 %all-to-all-start.2 = ((bf16[128,4,2048]{2,0,1:T(8,128)(2,1)}), bf16[128,4,2048]{2,0,1:T(8,128)(2,1)}, u32[]{:S(2)}, u32[]{:S(2)}) async-start(bf16[128,4,2048]{2,0,1:T(8,128)(2,1)} %bitcast.281), calls=%async_computation.4 | async-start | bytes 4194304 | tf_op jit(solution)/shard_map/all_to_all | solution.py:187
  2290.9 87.9 %reduce-scatter.18.cloned.1.call-start = ((), (), s32[]{:S(2)}) async-start(), calls=%async_computation.19 | async-start | bytes 1179648
  2292.3 228.6 %reduce-scatter.14.cloned.1.call-start = ((), (), s32[]{:S(2)}) async-start(), calls=%async_computation.16 | async-start | bytes 28311552 | tf_op jit(solution)/shard_map/reduce_scatter | solution.py:190
  2292.8 10.4 copy-start.34
  2339.1 10.2 copy-start.11
  2339.1 10.2 copy-start.12
  2363.4 521.0 %reduce-scatter.12.cloned.1.call-start = ((), (), s32[]{:S(2)}) async-start(), calls=%async_computation.14 | async-start | bytes 17301504 | tf_op jit(solution)/shard_map/reduce_scatter | solution.py:297
  2376.3 759.4 %reduce-scatter.10.cloned.1.call-start = ((), (), s32[]{:S(2)}) async-start(), calls=%async_computation.13 | async-start | bytes 25952256 | tf_op jit(solution)/shard_map/reduce_scatter | solution.py:296
  2377.4 18.9 copy-start.19
  2397.6 17.3 copy-start.20
  2414.9 9.4 copy-start.33
  (28 other events, 80.5 us)
Sparse Core Ops, SparseCore 0:
  9.5 220.9 all-gather.8
  238.4 21.5 all-gather.10
  262.5 23.3 all-gather.12
  287.3 149.5 all-gather.14
  438.4 1658.0 all-gather.16
  2098.4 43.8 all-gather.18
  2143.9 83.2 all-gather.20
  2282.9 37.2 reduce-scatter.15
  2323.9 35.9 reduce-scatter.17
  2363.5 157.3 reduce-scatter.13
  2523.8 360.6 reduce-scatter.11
  2891.3 244.3 reduce-scatter.9
where the time goes:
time: 3150 us; the launch traced here: 3140 us
  waiting for transfers between devices  2750 us (87%)
  matrix products  241 us (8%)
  other arithmetic  43.7 us (1%)
  blocking collectives  39.6 us (1%)
  local copies, waits for them, and re-layouts  38.9 us (1%)
    all_gather x1, waiting for transfers between devices, body(): weight_piece = lax.all_gather(ffn_weight, 'fsdp', axis=2, tiled=True)  1650 us
    reduce_scatter x1, waiting for transfers between devices, body(): lax.psum_scatter(out_term, ('ctx', 'fsdp'), scatter_dimension=0, tiled=True)  358 us
    reduce_scatter x1, waiting for transfers between devices, body(): lax.psum_scatter(qkv_term, ('ctx', 'fsdp'), scatter_dimension=0, tiled=True)  251 us
    all_gather x1, waiting for transfers between devices, body(): lax.all_gather(qkv_weight, 'fsdp', axis=0, tiled=True)  220 us
    all_gather x1, waiting for transfers between devices, body(): lax.all_gather(out_weight, 'fsdp', axis=0, tiled=True)  114 us
  transfers between devices with their start and end apart: 15, of which 11 were waited for; matrix products, arithmetic and copies ran while one was open for 10% of the time, Pallas kernels for 0%

commit v1 on v0

--- a/solution.py
+++ b/solution.py
@@ -10,6 +10,12 @@
 NORM_EPS = 1e-05
 ROPE_BASE = 500000.0
 block_rows = 512
+
+
+def in_order(blocks, dim):
+    blocks = jnp.moveaxis(blocks, 0, dim)
+    shape = blocks.shape
+    return blocks.reshape(*shape[:dim], shape[dim] * shape[dim + 1], *shape[dim + 2 :])
 
 
 def rotate(values, token_places):
@@ -149,7 +155,14 @@
         lax.all_gather(normed_two, "fsdp", axis=0, tiled=True),
         lax.all_gather(grad_in, "fsdp", axis=0, tiled=True),
     )
-    weight_piece = lax.all_gather(ffn_weight, "fsdp", axis=2, tiled=True)
+    size = lax.axis_size("fsdp")
+    right = [(i, (i + 1) % size) for i in range(size)]
+    blocks = [ffn_weight]
+    while len(blocks) < size:
+        blocks.append(lax.ppermute(blocks[-1], "fsdp", right))
+    index = lax.axis_index("fsdp")
+    blocks = jnp.stack(blocks)[(index - jnp.arange(size)) % size]
+    weight_piece = in_order(blocks, 2)
     gate_part = jnp.dot(normed_two, weight_piece[:, 0, :], preferred_element_type=jnp.float32)
     up_part = jnp.dot(normed_two, weight_piece[:, 1, :], preferred_element_type=jnp.float32)
     act_part = (gate_part * jax.nn.sigmoid(gate_part) * up_part).astype(jnp.bfloat16)

time: 3150 us -> 5250 us (1.67)
  waiting for transfers between devices: 2750 us -> 3510 us
  starting transfers between devices: 15.4 us -> 774 us
  local copies, waits for them, and re-layouts: 38.9 us -> 555 us
  other arithmetic: 43.7 us -> 110 us
    ppermute x0 -> x3, waiting for transfers between devices: none -> 2590 us  [body(): blocks.append(lax.ppermute(blocks[-1], 'fsdp', right))]
    all_gather x1, waiting for transfers between devices: 1650 us -> 0.01 us  [body(): weight_piece = lax.all_gather(ffn_weight, 'fsdp', axis=2, tiled=True)]
    ppermute x0 -> x3, starting transfers between devices: none -> 759 us  [body(): blocks.append(lax.ppermute(blocks[-1], 'fsdp', right))]
    gather x0 -> x129, local copies, waits for them, and re-layouts: none -> 391 us
    unnamed x58 -> x138, local copies, waits for them, and re-layouts: 16.5 us -> 137 us
    all_gather x1, waiting for transfers between devices: 114 us -> 0.01 us  [body(): lax.all_gather(out_weight, 'fsdp', axis=0, tiled=True)]
    another operation x2 -> x3, other arithmetic: 0.18 us -> 66.1 us  [the longest x1 65.9 us: body(): blocks = jnp.stack(blocks)[(index - jnp.arange(size)) % size]]
  transfers between devices with their start and end apart: 15 -> 18, of which waited for: 11 -> 10; matrix products, arithmetic and copies ran while one was open for 10% -> 16% of each run, Pallas kernels for 0% -> 0%
where the time goes in v1:
time: 5250 us; the launch traced here: 5240 us
  waiting for transfers between devices  3510 us (67%)
  starting transfers between devices  774 us (15%)
  local copies, waits for them, and re-layouts  555 us (11%)
  matrix products  232 us (4%)
  other arithmetic  110 us (2%)
    ppermute x3, waiting for transfers between devices, body(): blocks.append(lax.ppermute(blocks[-1], 'fsdp', right))  2590 us
    ppermute x3, starting transfers between devices, body(): blocks.append(lax.ppermute(blocks[-1], 'fsdp', right))  759 us
    reduce_scatter x1, waiting for transfers between devices, body(): lax.psum_scatter(out_term, ('ctx', 'fsdp'), scatter_dimension=0, tiled=True)  358 us
    gather x128, local copies, waits for them, and re-layouts  327 us
    reduce_scatter x1, waiting for transfers between devices, body(): lax.psum_scatter(qkv_term, ('ctx', 'fsdp'), scatter_dimension=0, tiled=True)  251 us
    all_gather x1, waiting for transfers between devices, body(): lax.all_gather(qkv_weight, 'fsdp', axis=0, tiled=True)  220 us
    unnamed x138, local copies, waits for them, and re-layouts  137 us
  transfers between devices with their start and end apart: 18, of which 10 were waited for; matrix products, arithmetic and copies ran while one was open for 16% of the time, Pallas kernels for 0%

profile of v1, /device:TPU:0, one launch (start us, length us, event | category | flops | bytes accessed | tf_op | source)
XLA Modules:
  0.0 5239.1 jit_solution(15298496412748583732)
XLA Ops:
  10.9 219.6 %all-gather.9.cloned.1.call-done = bf16[2048,3072]{1,0:T(8,128)(2,1)} async-done(((bf16[512,3072]{1,0:T(8,128)(2,1)}), bf16[2048,3072]{1,0:T(8,128)(2,1)}) %all-gather.9.cloned.1.call-update) | async-done | bytes 12582928 | tf_op jit(solution)/shard_map/all_gather | solution.py:88
  240.3 986.7 %collective-permute-done = bf16[2048,3,2048]{2,0,1:T(8,128)(2,1)S(1)} collective-permute-done((bf16[2048,3,2048]{2,0,1:T(8,128)(2,1)}, bf16[2048,3,2048]{2,0,1:T(8,128)(2,1)S(1)}, u32[]{:S(2)}, u32[]{:S(2)}) %collective-permute-start) | collective-permute-done | bytes 25165856 | tf_op jit(solution)/shard_map/ppermute | solution.py:162
  1235.3 331.9 %collective-permute-start.1 = (bf16[2048,3,2048]{2,0,1:T(8,128)(2,1)S(1)}, bf16[2048,3,2048]{2,0,1:T(8,128)(2,1)}, u32[]{:S(2)}, u32[]{:S(2)}) collective-permute-start(bf16[2048,3,2048]{2,0,1:T(8,128)(2,1)S(1)} %collective-permute-done), channel_id=1, source_target_pairs={{0,1},{1,2},{2,3},{3,0},{4,5},{5,6},{6,7},{7,4},{8,9},{9,10},{10,1... | collective-permute-start | bytes 75497480 | tf_op jit(solution)/shard_map/ppermute | solution.py:162
  1567.2 1078.1 %collective-permute-done.1 = bf16[2048,3,2048]{2,0,1:T(8,128)(2,1)} collective-permute-done((bf16[2048,3,2048]{2,0,1:T(8,128)(2,1)S(1)}, bf16[2048,3,2048]{2,0,1:T(8,128)(2,1)}, u32[]{:S(2)}, u32[]{:S(2)}) %collective-permute-start.1) | collective-permute-done | bytes 25165856 | tf_op jit(solution)/shard_map/ppermute | solution.py:162
  2645.4 427.4 %collective-permute-start.2 = (bf16[2048,3,2048]{2,0,1:T(8,128)(2,1)}, bf16[2048,3,2048]{2,0,1:T(8,128)(2,1)}, u32[]{:S(2)}, u32[]{:S(2)}) collective-permute-start(bf16[2048,3,2048]{2,0,1:T(8,128)(2,1)} %collective-permute-done.1), channel_id=1, source_target_pairs={{0,1},{1,2},{2,3},{3,0},{4,5},{5,6},{6,7},{7,4},{8,9},{9,10},{10,1... | collective-permute-start | bytes 75497480 | tf_op jit(solution)/shard_map/ppermute | solution.py:162
  3076.8 31.8 while.56
  3121.4 528.2 %collective-permute-done.2 = bf16[2048,3,2048]{2,0,1:T(8,128)(2,1)} collective-permute-done((bf16[2048,3,2048]{2,0,1:T(8,128)(2,1)}, bf16[2048,3,2048]{2,0,1:T(8,128)(2,1)}, u32[]{:S(2)}, u32[]{:S(2)}) %collective-permute-start.2) | collective-permute-done | bytes 25165856 | tf_op jit(solution)/shard_map/ppermute | solution.py:162
  3649.7 65.9 %pad_maximum_fusion = bf16[4,2048,3,2048]{3,1,2,0:T(8,128)(2,1)} fusion(bf16[1,2048,3,2048]{3,1,2,0:T(8,128)(2,1)} %bitcast.15, bf16[1,2048,3,2048]{3,1,2,0:T(8,128)(2,1)} %bitcast.14, bf16[1,2048,3,2048]{3,1,2,0:T(8,128)(2,1)} %bitcast.326, bf16[1,2048,3,2048]{3,1,2,0:T(8,128)(2,1)} %bitcast.310), kind=kLoop, calls=%fused_computation.90 | loop fusion | flops 150994944 | bytes 201326592 | tf_op jit(solution)/shard_map/stack | solution.py:164
  3715.6 63.7 %fusion.76 = (bf16[4,256,3,2048]{3,1,2,0:T(8,128)(2,1)}, bf16[4,256,3,2048]{3,1,2,0:T(8,128)(2,1)}, bf16[4,256,3,2048]{3,1,2,0:T(8,128)(2,1)}, bf16[4,256,3,2048...) fusion(bf16[4,2048,3,2048]{3,1,2,0:T(8,128)(2,1)} %pad_maximum_, ...), kind=kLoop, calls=%fused_computation.210 | loop fusion | bytes 201326592 | tf_op jit(solution)/shard_map/gather | solution.py:164
  3785.0 40.8 while.48
  3842.0 40.8 while.49
  3888.4 40.9 while.50
  3935.0 41.0 while.51
  3981.7 40.8 while.52
  4028.1 41.2 while.53
  4074.9 40.9 while.54
  4121.5 40.9 while.55
  4162.5 12.2 constant_dynamic-update-slice_fusion.16
  4220.8 17.5 fusion.39
  4238.4 15.0 fusion.37
  4253.3 20.0 multiply_convert_fusion.1
  4281.9 17.3 fusion.35
  4299.3 17.7 multiply_reduce_fusion
  4337.6 36.0 while.57
  4408.7 27.3 all-to-all-done.2
  4446.5 14.2 pad_maximum_fusion.1
  4477.5 16.0 fusion.63
  4494.8 15.3 fusion.44
  4519.4 39.5 all-reduce.2
  4561.4 55.9 %reduce-scatter.14.cloned.1.call-done = bf16[256,3,2048]{2,0,1:T(8,128)(2,1)} async-done(((bf16[2048,3,2048]{2,0,1:T(8,128)(2,1)}), bf16[256,3,2048]{2,0,1:T(8,128)(2,1)}) %reduce-scatter.14.cloned.1.call-update) | async-done | bytes 3145744 | tf_op jit(solution)/shard_map/reduce_scatter | solution.py:203
  4622.7 358.1 %reduce-scatter.12.cloned.1.call-done = f32[64,2048]{1,0:T(8,128)} async-done(((f32[2048,2048]{1,0:T(8,128)}), f32[64,2048]{1,0:T(8,128)}) %reduce-scatter.12.cloned.1.call-update) | async-done | bytes 524304 | tf_op jit(solution)/shard_map/reduce_scatter | solution.py:310
  4980.9 251.3 %reduce-scatter.10.cloned.1.call-done = f32[64,3072]{1,0:T(8,128)} async-done(((f32[2048,3072]{1,0:T(8,128)}), f32[64,3072]{1,0:T(8,128)}) %reduce-scatter.10.cloned.1.call-update) | async-done | bytes 786448 | tf_op jit(solution)/shard_map/reduce_scatter | solution.py:309
  (444 shorter events, 644.1 us)
Async XLA Ops:
  7.2 223.3 %all-gather.9.cloned.1.call-start = ((), (), s32[]{:S(2)}) async-start(), calls=%async_computation.8 | async-start | bytes 15728640 | tf_op jit(solution)/shard_map/all_gather | solution.py:88
  7.9 3065.8 %all-gather.11.cloned.1.call-start = ((), (), s32[]{:S(2)}) async-start(), calls=%async_computation.9 | async-start | bytes 1179648 | tf_op jit(solution)/shard_map/all_gather | solution.py:141
  10.9 226.3 %copy-start.39 = (f32[128]{0:T(128)}, f32[128]{0:T(128)S(1)}, u32[]{:S(2)}) copy-start(f32[128]{0:T(128)S(1)} %add_rsqrt_fusion.1) | copy-start | bytes 1540
  238.3 2837.0 %all-gather.13.cloned.1.call-start = ((), (), s32[]{:S(2)}) async-start(), calls=%async_computation.10 | async-start | bytes 1179648 | tf_op jit(solution)/shard_map/all_gather | solution.py:142
  239.0 2872.5 %all-gather.15.cloned.1.call-start = ((), (), s32[]{:S(2)}) async-start(), calls=%async_computation.11 | async-start | bytes 10485760 | tf_op jit(solution)/shard_map/all_gather | solution.py:89
  239.6 2833.2 %copy-start.35 = (s32[16]{0:T(128)S(1)}, s32[16]{0:T(128)}, u32[]{:S(2)}) copy-start(s32[16]{0:T(128)} %param.16) | copy-start | bytes 196
  239.6 3998.7 %all-gather.17.cloned.1.call-start = ((), (), s32[]{:S(2)}) async-start(), calls=%async_computation.12 | async-start | bytes 125829120 | tf_op jit(solution)/shard_map/all_gather | solution.py:177
  240.2 4149.8 %all-gather.19.cloned.1.call-start = ((), (), s32[]{:S(2)}) async-start(), calls=%async_computation.15 | async-start | bytes 2621440 | tf_op jit(solution)/shard_map/all_gather | solution.py:155
  240.3 986.7 %collective-permute-start = (bf16[2048,3,2048]{2,0,1:T(8,128)(2,1)}, bf16[2048,3,2048]{2,0,1:T(8,128)(2,1)S(1)}, u32[]{:S(2)}, u32[]{:S(2)}) collective-permute-start(bf16[2048,3,2048]{2,0,1:T(8,128)(2,1)} %param.21), channel_id=1, source_target_pairs={{0,1},{1,2},{2,3},{3,0},{4,5},{5,6},{6,7},{7,4},{8,9},{9,10},{10,1... | collective-permute-start | bytes 75497480 | tf_op jit(solution)/shard_map/ppermute | solution.py:162
  1235.3 1410.0 %collective-permute-start.1 = (bf16[2048,3,2048]{2,0,1:T(8,128)(2,1)S(1)}, bf16[2048,3,2048]{2,0,1:T(8,128)(2,1)}, u32[]{:S(2)}, u32[]{:S(2)}) collective-permute-start(bf16[2048,3,2048]{2,0,1:T(8,128)(2,1)S(1)} %collective-permute-done), channel_id=1, source_target_pairs={{0,1},{1,2},{2,3},{3,0},{4,5},{5,6},{6,7},{7,4},{8,9},{9,10},{10,1... | collective-permute-start | bytes 75497480 | tf_op jit(solution)/shard_map/ppermute | solution.py:162
  2645.4 1004.3 %collective-permute-start.2 = (bf16[2048,3,2048]{2,0,1:T(8,128)(2,1)}, bf16[2048,3,2048]{2,0,1:T(8,128)(2,1)}, u32[]{:S(2)}, u32[]{:S(2)}) collective-permute-start(bf16[2048,3,2048]{2,0,1:T(8,128)(2,1)} %collective-permute-done.1), channel_id=1, source_target_pairs={{0,1},{1,2},{2,3},{3,0},{4,5},{5,6},{6,7},{7,4},{8,9},{9,10},{10,1... | collective-permute-start | bytes 75497480 | tf_op jit(solution)/shard_map/ppermute | solution.py:162
  3076.7 34.8 copy-start.12
  3108.6 607.0 %copy-start.2 = (bf16[128,8,4,64]{0,3,2,1:T(8,128)(2,1)}, bf16[128,8,4,64]{0,3,2,1:T(8,128)(2,1)S(1)}, u32[]{:S(2)}) copy-start(bf16[128,8,4,64]{0,3,2,1:T(8,128)(2,1)S(1)} %get-tuple-element.1526) | copy-start | bytes 1572868
  3108.6 607.0 %copy-start.5 = (bf16[1024,512]{0,1:T(8,128)(2,1)}, bf16[1024,512]{0,1:T(8,128)(2,1)S(1)}, u32[]{:S(2)}) copy-start(bf16[1024,512]{0,1:T(8,128)(2,1)S(1)} %get-tuple-element.1535) | copy-start | bytes 3145732
  3108.6 607.0 %copy-start.7 = (bf16[1024,512]{0,1:T(8,128)(2,1)}, bf16[1024,512]{0,1:T(8,128)(2,1)S(1)}, u32[]{:S(2)}) copy-start(bf16[1024,512]{0,1:T(8,128)(2,1)S(1)} %get-tuple-element.1536) | copy-start | bytes 3145732
  3108.6 607.0 %copy-start.28 = (f32[8,4,128]{2,1,0:T(4,128)}, f32[8,4,128]{2,1,0:T(4,128)S(1)}, u32[]{:S(2)}) copy-start(f32[8,4,128]{2,1,0:T(4,128)S(1)} %get-tuple-element.524) | copy-start | bytes 49156
  3108.6 607.0 %copy-start.33 = (s32[128]{0:T(128)}, s32[128]{0:T(128)S(1)}, u32[]{:S(2)}) copy-start(s32[128]{0:T(128)S(1)} %get-tuple-element.1565) | copy-start | bytes 1540
  3118.1 597.5 %copy-start.43 = (f32[128]{0:T(128)}, f32[128]{0:T(128)S(1)}, u32[]{:S(2)}) copy-start(f32[128]{0:T(128)S(1)} %add_rsqrt_fusion) | copy-start | bytes 1540
  3120.0 1288.7 %all-gather.21.cloned.1.call-start = ((), (), s32[]{:S(2)}) async-start(), calls=%async_computation.17 | async-start | bytes 2621440 | tf_op jit(solution)/shard_map/all_gather | solution.py:156
  4220.8 17.5 copy-start.27
  4273.4 25.9 copy-start.25
  4277.3 53.4 %all-to-all-start.1 = ((bf16[128,4,2048]{2,0,1:T(8,128)(2,1)}), bf16[128,4,2048]{2,0,1:T(8,128)(2,1)}, u32[]{:S(2)}, u32[]{:S(2)}) async-start(bf16[128,4,2048]{2,0,1:T(8,128)(2,1)} %bitcast.237), calls=%async_computation.3 | async-start | bytes 4194304 | tf_op jit(solution)/shard_map/all_to_all | solution.py:199
  4281.9 17.4 copy-start.15
  4281.9 17.4 copy-start.38
  4281.9 17.4 copy-start.44
  4330.7 53.0 %all-to-all-start = ((bf16[128,4,2048]{2,0,1:T(8,128)(2,1)}), bf16[128,4,2048]{2,0,1:T(8,128)(2,1)}, u32[]{:S(2)}, u32[]{:S(2)}) async-start(bf16[128,4,2048]{2,0,1:T(8,128)(2,1)} %bitcast.332), calls=%async_computation.2 | async-start | bytes 4194304 | tf_op jit(solution)/shard_map/all_to_all | solution.py:198
  4335.4 139.8 %reduce-scatter.16.cloned.1.call-start = ((), (), s32[]{:S(2)}) async-start(), calls=%async_computation.18 | async-start | bytes 1179648
  4383.7 52.3 all-to-all-start.2
  4388.2 88.3 %reduce-scatter.18.cloned.1.call-start = ((), (), s32[]{:S(2)}) async-start(), calls=%async_computation.19 | async-start | bytes 1179648
  4389.6 227.7 %reduce-scatter.14.cloned.1.call-start = ((), (), s32[]{:S(2)}) async-start(), calls=%async_computation.16 | async-start | bytes 28311552 | tf_op jit(solution)/shard_map/reduce_scatter | solution.py:203
  4460.7 520.1 %reduce-scatter.12.cloned.1.call-start = ((), (), s32[]{:S(2)}) async-start(), calls=%async_computation.14 | async-start | bytes 17301504 | tf_op jit(solution)/shard_map/reduce_scatter | solution.py:310
  4474.1 758.0 %reduce-scatter.10.cloned.1.call-start = ((), (), s32[]{:S(2)}) async-start(), calls=%async_computation.13 | async-start | bytes 25952256 | tf_op jit(solution)/shard_map/reduce_scatter | solution.py:309
  (57 other events, 369.9 us)
Sparse Core Ops, SparseCore 0:
  9.5 220.9 all-gather.8
  238.4 21.5 all-gather.10
  262.5 23.3 all-gather.12
  287.3 283.9 all-gather.14
  572.7 2504.5 all-gather.16
  3120.2 529.7 all-gather.18
  3651.5 41.5 all-gather.20
  4376.2 37.6 reduce-scatter.15
  4417.6 35.9 reduce-scatter.17
  4460.8 156.4 reduce-scatter.13
  4620.2 360.6 reduce-scatter.11
  4987.7 244.3 reduce-scatter.9
